TPU v7x, 32 devices: a whole 2x2x4 slice. The times are simulated.
32 devices in a mesh: pipe: 2 (over x), dp: 4 (over y, core), tensor: 4 (over z).
Axes of the slice: x: 2, y: 2, z: 4, core: 2. Of those that a mesh axis runs over, the one named last changes fastest.
Arguments:
- inputs: bfloat16 [4, 1024, 1024], P(None, ('dp', 'tensor')), may hold values from -6 to 6
- segments: int32 [4, 1024], P(None, 'dp'), may hold values from 0 to 7, never falling along the last dimension, each value on 1 to 256 neighbouring positions
- cotangent: bfloat16 [4, 1024, 1024], P(None, ('dp', 'tensor')), may hold values from -6 to 6
- w_qkv: bfloat16 [2, 1024, 3, 1024], P('pipe', 'dp', None, 'tensor'), may hold values from -0.1875 to 0.1875
- w_o: bfloat16 [2, 1024, 1024], P('pipe', 'tensor', 'dp'), may hold values from -1.5 to 1.5
- w_in: bfloat16 [2, 1024, 4096], P('pipe', 'dp', 'tensor'), may hold values from -0.1875 to 0.1875
- w_out: bfloat16 [2, 4096, 1024], P('pipe', 'tensor', 'dp'), may hold values from -0.09375 to 0.09375
- ln_gains: float32 [2, 2, 1024], P('pipe'), may hold values from 0.1 to 1.9
- model_biases: float32 [2, 6, 1024], P('pipe'), may hold values from -1 to 1
- hidden_bias: float32 [2, 4096], P('pipe'), may hold values from -2.5 to 2.5
Outputs:
- section_outputs: bfloat16 [2, 4, 1024, 1024], P('pipe', None, ('dp', 'tensor'))
- input_grads: bfloat16 [2, 4, 1024, 1024], P('pipe', None, ('dp', 'tensor'))
- grad_qkv: float32 [2, 1024, 3, 1024], P('pipe', 'dp', None, 'tensor')
- grad_o: float32 [2, 1024, 1024], P('pipe', 'tensor', 'dp')
- grad_in: float32 [2, 1024, 4096], P('pipe', 'dp', 'tensor')
- grad_out: float32 [2, 4096, 1024], P('pipe', 'tensor', 'dp')
- grad_gains: float32 [2, 2, 1024], P('pipe', None, ('dp', 'tensor'))
- grad_biases: float32 [2, 6, 1024], P('pipe', None, ('dp', 'tensor'))
- grad_hidden_bias: float32 [2, 4096], P('pipe', ('dp', 'tensor'))
Inputs may be any that keep to these rules, and one draw needn't show every extreme that they name: `segments`: segment numbers never fall along a micro-batch's 1024 tokens; a segment holds 1 to 256 tokens and some segment holds exactly 256.
All inputs are finite; a program needn't handle non-finite values.
Results may differ from a plain program's by a relative error of at most 0.028.
Values may be sent and summed in bfloat16 or wider, within the bound.
No kernel may reach another device: no remote copies, remote signals or barrier semaphores. Data moves between devices by JAX's collectives and lax.ppermute only.
A program may use at most 128 MiB of HBM per device.

v0:
```python
import jax
import jax.numpy as jnp
from jax import lax
from jax.sharding import PartitionSpec as P

HEAD_DIM = 64
NORM_EPS = 1e-12
MASKED = -1000000000.0
ROOT_HALF = 0.7071067811865476
INV_ROOT_TWOPI = 0.3989422804014327


def shifted(block, axis, distance):
    devices = range(lax.axis_size(axis))
    route = [(i - distance, i) for i in devices if i - distance in devices]
    return lax.ppermute(block, axis, route)


def dot_rows(left_side, right_side):
    return lax.dot_general(
        left_side, right_side, (((0,), (0,)), ((), ())), preferred_element_type=jnp.float32
    )


def dot_cols(left_side, right_side):
    return lax.dot_general(
        left_side, right_side, (((1,), (1,)), ((), ())), preferred_element_type=jnp.float32
    )


def norm_forward(values, gain_row, shift_row):
    center = values - jnp.mean(values, axis=-1, keepdims=True)
    spread = jnp.mean(center * center, axis=-1, keepdims=True)
    inverse = lax.rsqrt(spread + NORM_EPS)
    scaled = center * inverse
    return (scaled * gain_row + shift_row, scaled, inverse)


def norm_backward(upstream, scaled, inverse, gain_row):
    weighted = upstream * gain_row
    inner_term = (
        weighted
        - jnp.mean(weighted, axis=-1, keepdims=True)
        - scaled * jnp.mean(weighted * scaled, axis=-1, keepdims=True)
    )
    return (inverse * inner_term, jnp.sum(upstream * scaled, axis=0), jnp.sum(upstream, axis=0))


def gelu_slope(values):
    return 0.5 * (1.0 + lax.erf(values * ROOT_HALF)) + values * INV_ROOT_TWOPI * jnp.exp(
        -0.5 * values * values
    )


def masked_scores(query_seq, key_seq, label_seq):
    scores = jnp.einsum(
        "qhe,khe->hqk", query_seq, key_seq, preferred_element_type=jnp.float32
    ) * HEAD_DIM ** (-0.5)
    allowed = label_seq[:, None] == label_seq[None, :]
    return jnp.where(allowed[None], scores, MASKED)


def attend(queries, key_rows, value_rows, labels):
    row_count, local_width = queries.shape
    heads_here = local_width // HEAD_DIM
    shaped = [
        member.reshape(1, row_count, heads_here, HEAD_DIM)
        for member in (queries, key_rows, value_rows)
    ]

    def one_sequence(pieces):
        query_seq, key_seq, value_seq, label_seq = pieces
        scores = masked_scores(query_seq, key_seq, label_seq)
        largest = jnp.max(scores, axis=-1, keepdims=True)
        total_mass = jnp.sum(jnp.exp(scores - largest), axis=-1, keepdims=True)
        log_total = largest + jnp.log(total_mass)
        weights = jnp.exp(scores - log_total).astype(jnp.bfloat16)
        context = jnp.einsum("hqk,khe->qhe", weights, value_seq, preferred_element_type=jnp.float32)
        return (context.astype(jnp.bfloat16), log_total[..., 0])

    context, log_total = lax.map(
        one_sequence, (shaped[0], shaped[1], shaped[2], labels.reshape(1, row_count))
    )
    return (context.reshape(row_count, local_width), log_total)


def attend_back(queries, key_rows, value_rows, labels, log_total, grad_context):
    row_count, local_width = queries.shape
    heads_here = local_width // HEAD_DIM
    shaped = [
        member.reshape(1, row_count, heads_here, HEAD_DIM)
        for member in (queries, key_rows, value_rows, grad_context)
    ]
    score_scale = HEAD_DIM ** (-0.5)

    def one_sequence(pieces):
        query_seq, key_seq, value_seq, label_seq, total_seq, grad_seq = pieces
        scores = masked_scores(query_seq, key_seq, label_seq)
        weights = jnp.exp(scores - total_seq[..., None])
        weights_low = weights.astype(jnp.bfloat16)
        grad_weights = jnp.einsum(
            "qhe,khe->hqk", grad_seq, value_seq, preferred_element_type=jnp.float32
        )
        inner_term = jnp.sum(weights * grad_weights, axis=-1, keepdims=True)
        grad_scores = (weights * (grad_weights - inner_term)).astype(jnp.bfloat16)
        grad_query = (
            jnp.einsum("hqk,khe->qhe", grad_scores, key_seq, preferred_element_type=jnp.float32)
            * score_scale
        )
        grad_keys = (
            jnp.einsum("hqk,qhe->khe", grad_scores, query_seq, preferred_element_type=jnp.float32)
            * score_scale
        )
        grad_values = jnp.einsum(
            "hqk,qhe->khe", weights_low, grad_seq, preferred_element_type=jnp.float32
        )
        return jnp.stack((grad_query, grad_keys, grad_values), axis=1).astype(jnp.bfloat16)

    stacked = lax.map(
        one_sequence,
        (shaped[0], shaped[1], shaped[2], labels.reshape(1, row_count), log_total, shaped[3]),
    )
    return stacked.reshape(row_count, 3, local_width)


def layer_forward(current, labels, weights, vectors):
    w_qkv, w_o, w_in, w_out = weights
    gains, biases, query_bias, value_bias, local_hidden_bias = vectors
    gathered = lax.all_gather(current, "tensor", axis=0, tiled=True)
    projected = jnp.einsum("gd,dcn->gcn", gathered, w_qkv, preferred_element_type=jnp.float32)
    queries = (projected[:, 0] + query_bias).astype(jnp.bfloat16)
    key_rows = projected[:, 1].astype(jnp.bfloat16)
    value_rows = (projected[:, 2] + value_bias).astype(jnp.bfloat16)
    context, log_total = attend(queries, key_rows, value_rows, labels)
    partial_value = jnp.dot(context, w_o, preferred_element_type=jnp.float32)
    mixed_rows = lax.psum_scatter(partial_value, "tensor", scatter_dimension=0, tiled=True)
    normed, scaled_one, inverse_one = norm_forward(
        current.astype(jnp.float32) + mixed_rows + biases[2], gains[0], biases[3]
    )
    spread_rows = lax.all_gather(normed.astype(jnp.bfloat16), "tensor", axis=0, tiled=True)
    hidden = jnp.dot(spread_rows, w_in, preferred_element_type=jnp.float32) + local_hidden_bias
    active = jax.nn.gelu(hidden, approximate=False).astype(jnp.bfloat16)
    partial_out = jnp.dot(active, w_out, preferred_element_type=jnp.float32)
    branch = lax.psum_scatter(
        partial_out.astype(jnp.bfloat16), "tensor", scatter_dimension=0, tiled=True
    ).astype(jnp.float32)
    final_rows, scaled_two, inverse_two = norm_forward(
        normed + branch + biases[4], gains[1], biases[5]
    )
    kept_state = (
        gathered,
        queries,
        key_rows,
        value_rows,
        context,
        log_total,
        scaled_one,
        inverse_one,
        spread_rows,
        hidden,
        active,
        scaled_two,
        inverse_two,
    )
    return (final_rows.astype(jnp.bfloat16), kept_state)


def layer_backward(upstream, kept_state, labels, weights, gains):
    (
        gathered,
        queries,
        key_rows,
        value_rows,
        context,
        log_total,
        scaled_one,
        inverse_one,
        spread_rows,
        hidden,
        active,
        scaled_two,
        inverse_two,
    ) = kept_state
    w_qkv, w_o, w_in, w_out = weights
    grad_second, gain_two, shift_two = norm_backward(upstream, scaled_two, inverse_two, gains[1])
    grad_feed = lax.all_gather(grad_second.astype(jnp.bfloat16), "tensor", axis=0, tiled=True)
    grad_active = dot_cols(grad_feed, w_out)
    grad_w_out = dot_rows(active, grad_feed)
    grad_hidden = (grad_active * gelu_slope(hidden)).astype(jnp.bfloat16)
    grad_w_in = dot_rows(spread_rows, grad_hidden)
    grad_spread = dot_cols(grad_hidden, w_in)
    grad_normed = grad_second + lax.psum_scatter(
        grad_spread.astype(jnp.bfloat16), "tensor", scatter_dimension=0, tiled=True
    ).astype(jnp.float32)
    grad_first, gain_one, shift_one = norm_backward(grad_normed, scaled_one, inverse_one, gains[0])
    grad_mix = lax.all_gather(grad_first.astype(jnp.bfloat16), "tensor", axis=0, tiled=True)
    grad_context = dot_cols(grad_mix, w_o).astype(jnp.bfloat16)
    grad_w_o = dot_rows(context, grad_mix)
    grad_project = attend_back(queries, key_rows, value_rows, labels, log_total, grad_context)
    grad_w_qkv = jnp.einsum(
        "gd,gcn->dcn", gathered, grad_project, preferred_element_type=jnp.float32
    )
    grad_gathered = jnp.einsum(
        "gcn,dcn->gd", grad_project, w_qkv, preferred_element_type=jnp.float32
    )
    grad_current = grad_first + lax.psum_scatter(
        grad_gathered.astype(jnp.bfloat16), "tensor", scatter_dimension=0, tiled=True
    ).astype(jnp.float32)
    column_sums = jnp.sum(grad_project.astype(jnp.float32), axis=0)
    gain_grads = jnp.stack([gain_one, gain_two])
    row_grads = jnp.stack(
        [jnp.sum(grad_first, axis=0), shift_one, jnp.sum(grad_second, axis=0), shift_two]
    )
    local_grads = jnp.stack([column_sums[0], column_sums[2]])
    hidden_grads = jnp.sum(grad_hidden.astype(jnp.float32), axis=0)
    return (
        grad_current,
        (grad_w_qkv, grad_w_o, grad_w_in, grad_w_out),
        (gain_grads, row_grads, local_grads, hidden_grads),
    )


def body(inputs, segments, cotangent, w_qkv, w_o, w_in, w_out, ln_gains, model_biases, hidden_bias):
    section_first = lax.axis_index("pipe") == 0
    column = lax.axis_index("tensor")
    micro_count = inputs.shape[0]
    row_count = inputs.shape[1]
    model_width = model_biases.shape[-1]
    hidden_width = hidden_bias.shape[-1]
    width_local = w_qkv.shape[-1]
    hidden_local = w_in.shape[-1]
    gains = ln_gains[0]
    biases = model_biases[0]
    query_bias = lax.dynamic_slice_in_dim(biases[0], column * width_local, width_local)
    value_bias = lax.dynamic_slice_in_dim(biases[1], column * width_local, width_local)
    local_hidden_bias = lax.dynamic_slice_in_dim(
        hidden_bias[0], column * hidden_local, hidden_local
    )
    vectors = (gains, biases, query_bias, value_bias, local_hidden_bias)
    shards = (w_qkv[0], w_o[0], w_in[0], w_out[0])
    blank_rows = jnp.zeros((row_count, model_width), jnp.bfloat16)
    incoming = blank_rows
    returning = blank_rows
    kept_list = []
    forward_list = []
    backward_list = []
    weight_totals = None
    vector_totals = None
    for tick_index in range(micro_count + 2):
        weights = (
            lax.all_gather(shards[0], "dp", axis=0, tiled=True),
            lax.all_gather(shards[1], "dp", axis=1, tiled=True),
            lax.all_gather(shards[2], "dp", axis=0, tiled=True),
            lax.all_gather(shards[3], "dp", axis=1, tiled=True),
        )
        own_rows = inputs[tick_index] if tick_index < micro_count else blank_rows
        current = jnp.where(section_first, own_rows, incoming)
        labels_forward = jnp.where(
            section_first,
            segments[min(tick_index, micro_count - 1)],
            segments[max(min(tick_index - 1, micro_count - 1), 0)],
        )
        final_rows, kept_state = layer_forward(current, labels_forward, weights, vectors)
        forward_list.append(final_rows)
        incoming = shifted(final_rows, "pipe", 1)
        given_grad = cotangent[tick_index - 1] if 1 <= tick_index <= micro_count else blank_rows
        upstream = jnp.where(section_first, returning, given_grad).astype(jnp.float32)
        earlier = kept_list[tick_index - 2] if tick_index >= 2 else kept_state
        chosen_state = jax.tree.map(
            lambda first_item, second_item: jnp.where(section_first, first_item, second_item),
            earlier,
            kept_state,
        )
        labels_backward = jnp.where(
            section_first,
            segments[max(min(tick_index - 2, micro_count - 1), 0)],
            segments[max(min(tick_index - 1, micro_count - 1), 0)],
        )
        grad_current, weight_grads, vector_grads = layer_backward(
            upstream, chosen_state, labels_backward, weights, gains
        )
        if tick_index == 0:
            weight_totals = weight_grads
            vector_totals = vector_grads
        else:
            weight_totals = jax.tree.map(jnp.add, weight_totals, weight_grads)
            vector_totals = jax.tree.map(jnp.add, vector_totals, vector_grads)
        grad_low = grad_current.astype(jnp.bfloat16)
        backward_list.append(grad_low)
        returning = shifted(grad_low, "pipe", -1)
        kept_list.append(kept_state)
    summed = (
        lax.psum_scatter(
            weight_totals[0].astype(jnp.bfloat16), "dp", scatter_dimension=0, tiled=True
        ).astype(jnp.float32),
        lax.psum_scatter(
            weight_totals[1].astype(jnp.bfloat16), "dp", scatter_dimension=1, tiled=True
        ).astype(jnp.float32),
        lax.psum_scatter(
            weight_totals[2].astype(jnp.bfloat16), "dp", scatter_dimension=0, tiled=True
        ).astype(jnp.float32),
        lax.psum_scatter(
            weight_totals[3].astype(jnp.bfloat16), "dp", scatter_dimension=1, tiled=True
        ).astype(jnp.float32),
    )
    gain_grads, row_grads, local_grads, hidden_grads = vector_totals
    zero_index = jnp.zeros((), jnp.int32)
    placed = lax.dynamic_update_slice(
        jnp.zeros((2, model_width), jnp.float32), local_grads, (zero_index, column * width_local)
    )
    bias_full = jnp.concatenate([placed, row_grads], axis=0)
    hidden_full = lax.dynamic_update_slice(
        jnp.zeros((hidden_width,), jnp.float32), hidden_grads, (column * hidden_local,)
    )
    vector_sums = (
        lax.psum_scatter(gain_grads, ("dp", "tensor"), scatter_dimension=1, tiled=True),
        lax.psum_scatter(bias_full, ("dp", "tensor"), scatter_dimension=1, tiled=True),
        lax.psum_scatter(hidden_full, ("dp", "tensor"), scatter_dimension=0, tiled=True),
    )
    section_rows = jnp.stack(
        [
            jnp.where(section_first, forward_list[batch_index], forward_list[batch_index + 1])
            for batch_index in range(micro_count)
        ]
    )[None]
    grad_rows = jnp.stack(
        [
            jnp.where(section_first, backward_list[batch_index + 2], backward_list[batch_index + 1])
            for batch_index in range(micro_count)
        ]
    )[None]
    return (
        section_rows,
        grad_rows,
        summed[0][None],
        summed[1][None],
        summed[2][None],
        summed[3][None],
        vector_sums[0][None],
        vector_sums[1][None],
        vector_sums[2][None],
    )


def solution(mesh):
    return jax.shard_map(
        body,
        mesh=mesh,
        in_specs=(
            P(None, ("dp", "tensor"), None),
            P(None, "dp"),
            P(None, ("dp", "tensor"), None),
            P("pipe", "dp", None, "tensor"),
            P("pipe", "tensor", "dp"),
            P("pipe", "dp", "tensor"),
            P("pipe", "tensor", "dp"),
            P("pipe", None, None),
            P("pipe", None, None),
            P("pipe", None),
        ),
        out_specs=(
            P("pipe", None, ("dp", "tensor"), None),
            P("pipe", None, ("dp", "tensor"), None),
            P("pipe", "dp", None, "tensor"),
            P("pipe", "tensor", "dp"),
            P("pipe", "dp", "tensor"),
            P("pipe", "tensor", "dp"),
            P("pipe", None, ("dp", "tensor")),
            P("pipe", None, ("dp", "tensor")),
            P("pipe", ("dp", "tensor")),
        ),
        check_vma=False,
    )
```

profile of v0, /device:TPU:0, one launch (start us, length us, event | category | flops | bytes accessed | tf_op | source)
XLA Modules:
  0.0 1324.4 jit_solution(16337392418680728141)
XLA Ops:
  11.8 17.4 %all-gather = bf16[1,256,1024]{2,1,0:T(8,128)(2,1)S(1)} all-gather(bf16[1,64,1024]{2,1,0:T(8,128)(2,1)S(1)} %slice_select_fusion), channel_id=2, replica_groups=mesh['pipe'=2,'dp'=4,'tensor'=4] {'tensor'}, dimensions={1}, use_global_device_ids=true | all-gather | bytes 655360 | tf_op jit(solution)/shard_map/all_gather | solution.py:129
  43.2 27.1 %reduce-scatter.35.cloned.1.call-done = f32[64,1024]{1,0:T(8,128)} async-done(((f32[256,1024]{1,0:T(8,128)}), f32[64,1024]{1,0:T(8,128)}) %reduce-scatter.35.cloned.1.call-update) | async-done | bytes 262160 | tf_op jit(solution)/shard_map/reduce_scatter | solution.py:136
  73.6 15.9 %all_gather.107 = bf16[256,1024]{1,0:T(8,128)(2,1)S(1)} all-gather(bf16[64,1024]{1,0:T(8,128)(2,1)S(1)} %get-tuple-element.418), channel_id=1, replica_groups=mesh['pipe'=2,'dp'=4,'tensor'=4] {'tensor'}, dimensions={0}, use_global_device_ids=true | all-gather | bytes 655360 | tf_op jit(solution)/shard_map/all_gather | solution.py:140
  98.4 18.8 %all-gather.13.cloned.1.call-done = bf16[1,1024,1024]{2,1,0:T(8,128)(2,1)} async-done(((bf16[1,1024,256]{2,1,0:T(8,128)(2,1)}), bf16[1,1024,1024]{2,1,0:T(8,128)(2,1)}) %all-gather.13.cloned.1.call-update) | async-done | bytes 2097168 | tf_op jit(solution)/shard_map/all_gather | solution.py:254
  121.6 20.6 %reduce-scatter.37.cloned.1.call-done = bf16[64,1024]{1,0:T(8,128)(2,1)} async-done(((bf16[256,1024]{1,0:T(8,128)(2,1)}), bf16[64,1024]{1,0:T(8,128)(2,1)}) %reduce-scatter.37.cloned.1.call-update) | async-done | bytes 131088 | tf_op jit(solution)/shard_map/reduce_scatter | solution.py:144
  167.5 19.8 %reduce-scatter.55.cloned.1.call-done = bf16[64,1024]{1,0:T(8,128)(2,1)} async-done(((bf16[256,1024]{1,0:T(8,128)(2,1)}), bf16[64,1024]{1,0:T(8,128)(2,1)}) %reduce-scatter.55.cloned.1.call-update) | async-done | bytes 131088 | tf_op jit(solution)/shard_map/reduce_scatter | solution.py:192
  218.4 25.7 %reduce-scatter.39.cloned.1.call-done = f32[64,1024]{1,0:T(8,128)} async-done(((f32[256,1024]{1,0:T(8,128)}), f32[64,1024]{1,0:T(8,128)}) %reduce-scatter.39.cloned.1.call-update) | async-done | bytes 262160 | tf_op jit(solution)/shard_map/reduce_scatter | solution.py:136
  249.5 16.0 %all_gather.119 = bf16[256,1024]{1,0:T(8,128)(2,1)S(1)} all-gather(bf16[64,1024]{1,0:T(8,128)(2,1)S(1)} %convert_element_type.638), channel_id=1, replica_groups=mesh['pipe'=2,'dp'=4,'tensor'=4] {'tensor'}, dimensions={0}, use_global_device_ids=true | all-gather | bytes 655360 | tf_op jit(solution)/shard_map/all_gather | solution.py:196
  317.2 16.9 %reduce-scatter.57.cloned.1.call-done = bf16[64,1024]{1,0:T(8,128)(2,1)} async-done(((bf16[256,1024]{1,0:T(8,128)(2,1)}), bf16[64,1024]{1,0:T(8,128)(2,1)}) %reduce-scatter.57.cloned.1.call-update) | async-done | bytes 131088 | tf_op jit(solution)/shard_map/reduce_scatter | solution.py:206
  356.9 15.9 %all_gather.120 = bf16[256,1024]{1,0:T(8,128)(2,1)S(1)} all-gather(bf16[64,1024]{1,0:T(8,128)(2,1)S(1)} %get-tuple-element.388), channel_id=1, replica_groups=mesh['pipe'=2,'dp'=4,'tensor'=4] {'tensor'}, dimensions={0}, use_global_device_ids=true | all-gather | bytes 655360 | tf_op jit(solution)/shard_map/all_gather | solution.py:186
  399.1 26.2 %reduce-scatter.43.cloned.1.call-done = f32[64,1024]{1,0:T(8,128)} async-done(((f32[256,1024]{1,0:T(8,128)}), f32[64,1024]{1,0:T(8,128)}) %reduce-scatter.43.cloned.1.call-update) | async-done | bytes 262160 | tf_op jit(solution)/shard_map/reduce_scatter | solution.py:136
  429.2 16.1 %all_gather.113 = bf16[256,1024]{1,0:T(8,128)(2,1)S(1)} all-gather(bf16[64,1024]{1,0:T(8,128)(2,1)S(1)} %get-tuple-element.477), channel_id=1, replica_groups=mesh['pipe'=2,'dp'=4,'tensor'=4] {'tensor'}, dimensions={0}, use_global_device_ids=true | all-gather | bytes 655360 | tf_op jit(solution)/shard_map/all_gather | solution.py:140
  452.7 18.0 %all_gather.121 = bf16[256,1024]{1,0:T(8,128)(2,1)S(1)} all-gather(bf16[64,1024]{1,0:T(8,128)(2,1)S(1)} %convert_element_type.649), channel_id=1, replica_groups=mesh['pipe'=2,'dp'=4,'tensor'=4] {'tensor'}, dimensions={0}, use_global_device_ids=true | all-gather | bytes 655360 | tf_op jit(solution)/shard_map/all_gather | solution.py:196
  490.1 17.9 %all_gather.114 = bf16[256,1024]{1,0:T(8,128)(2,1)S(1)} all-gather(bf16[64,1024]{1,0:T(8,128)(2,1)S(1)} %bitcast_select_fusion.6), channel_id=1, replica_groups=mesh['pipe'=2,'dp'=4,'tensor'=4] {'tensor'}, dimensions={0}, use_global_device_ids=true | all-gather | bytes 655360 | tf_op jit(solution)/shard_map/all_gather | solution.py:129
  523.9 20.3 %all_gather.122 = bf16[256,1024]{1,0:T(8,128)(2,1)S(1)} all-gather(bf16[64,1024]{1,0:T(8,128)(2,1)S(1)} %get-tuple-element.384), channel_id=1, replica_groups=mesh['pipe'=2,'dp'=4,'tensor'=4] {'tensor'}, dimensions={0}, use_global_device_ids=true | all-gather | bytes 655360 | tf_op jit(solution)/shard_map/all_gather | solution.py:186
  551.2 20.7 %reduce-scatter.63.cloned.1.call-done = bf16[64,1024]{1,0:T(8,128)(2,1)} async-done(((bf16[256,1024]{1,0:T(8,128)(2,1)}), bf16[64,1024]{1,0:T(8,128)(2,1)}) %reduce-scatter.63.cloned.1.call-update) | async-done | bytes 131088 | tf_op jit(solution)/shard_map/reduce_scatter | solution.py:192
  596.4 20.2 %reduce-scatter.49.cloned.1.call-done = bf16[64,1024]{1,0:T(8,128)(2,1)} async-done(((bf16[256,1024]{1,0:T(8,128)(2,1)}), bf16[64,1024]{1,0:T(8,128)(2,1)}) %reduce-scatter.49.cloned.1.call-update) | async-done | bytes 131088 | tf_op jit(solution)/shard_map/reduce_scatter | solution.py:144
  645.1 27.3 %reduce-scatter.51.cloned.1.call-done = f32[64,1024]{1,0:T(8,128)} async-done(((f32[256,1024]{1,0:T(8,128)}), f32[64,1024]{1,0:T(8,128)}) %reduce-scatter.51.cloned.1.call-update) | async-done | bytes 262160 | tf_op jit(solution)/shard_map/reduce_scatter | solution.py:136
  675.2 16.0 %all_gather.117 = bf16[256,1024]{1,0:T(8,128)(2,1)S(1)} all-gather(bf16[64,1024]{1,0:T(8,128)(2,1)S(1)} %get-tuple-element.475), channel_id=1, replica_groups=mesh['pipe'=2,'dp'=4,'tensor'=4] {'tensor'}, dimensions={0}, use_global_device_ids=true | all-gather | bytes 655360 | tf_op jit(solution)/shard_map/all_gather | solution.py:140
  698.4 18.1 %all_gather.123 = bf16[256,1024]{1,0:T(8,128)(2,1)S(1)} all-gather(bf16[64,1024]{1,0:T(8,128)(2,1)S(1)} %convert_element_type.661), channel_id=1, replica_groups=mesh['pipe'=2,'dp'=4,'tensor'=4] {'tensor'}, dimensions={0}, use_global_device_ids=true | all-gather | bytes 655360 | tf_op jit(solution)/shard_map/all_gather | solution.py:196
  736.3 17.8 %all_gather.128 = bf16[256,1024]{1,0:T(8,128)(2,1)S(1)} all-gather(bf16[64,1024]{1,0:T(8,128)(2,1)S(1)} %broadcast_select_fusion.9), channel_id=1, replica_groups=mesh['pipe'=2,'dp'=4,'tensor'=4] {'tensor'}, dimensions={0}, use_global_device_ids=true | all-gather | bytes 655360 | tf_op jit(solution)/shard_map/all_gather | solution.py:129
  769.7 21.1 %all_gather.124 = bf16[256,1024]{1,0:T(8,128)(2,1)S(1)} all-gather(bf16[64,1024]{1,0:T(8,128)(2,1)S(1)} %get-tuple-element.377), channel_id=1, replica_groups=mesh['pipe'=2,'dp'=4,'tensor'=4] {'tensor'}, dimensions={0}, use_global_device_ids=true | all-gather | bytes 655360 | tf_op jit(solution)/shard_map/all_gather | solution.py:186
  798.7 19.1 %reduce-scatter.67.cloned.1.call-done = bf16[64,1024]{1,0:T(8,128)(2,1)} async-done(((bf16[256,1024]{1,0:T(8,128)(2,1)}), bf16[64,1024]{1,0:T(8,128)(2,1)}) %reduce-scatter.67.cloned.1.call-update) | async-done | bytes 131088 | tf_op jit(solution)/shard_map/reduce_scatter | solution.py:192
  847.5 18.1 %all_gather.129 = bf16[256,1024]{1,0:T(8,128)(2,1)S(1)} all-gather(bf16[64,1024]{1,0:T(8,128)(2,1)} %get-tuple-element.464), channel_id=1, replica_groups=mesh['pipe'=2,'dp'=4,'tensor'=4] {'tensor'}, dimensions={0}, use_global_device_ids=true | all-gather | bytes 655360 | tf_op jit(solution)/shard_map/all_gather | solution.py:140
  881.6 20.7 %all_gather.126 = bf16[256,1024]{1,0:T(8,128)(2,1)S(1)} all-gather(bf16[64,1024]{1,0:T(8,128)(2,1)S(1)} %get-tuple-element.370), channel_id=1, replica_groups=mesh['pipe'=2,'dp'=4,'tensor'=4] {'tensor'}, dimensions={0}, use_global_device_ids=true | all-gather | bytes 655360 | tf_op jit(solution)/shard_map/all_gather | solution.py:186
  936.4 15.6 %all_gather.127 = bf16[256,1024]{1,0:T(8,128)(2,1)S(1)} all-gather(bf16[64,1024]{1,0:T(8,128)(2,1)S(1)} %convert_element_type.685), channel_id=1, replica_groups=mesh['pipe'=2,'dp'=4,'tensor'=4] {'tensor'}, dimensions={0}, use_global_device_ids=true | all-gather | bytes 655360 | tf_op jit(solution)/shard_map/all_gather | solution.py:196
  1102.5 58.1 %all-reduce = f32[4096]{0:T(1024)S(1)} all-reduce(f32[4096]{0:T(1024)S(1)} %add_dynamic-update-slice_fusion), channel_id=37, replica_groups=mesh['pipe'=2,'dp'=4,'tensor'=4] {'dp','tensor'}, use_global_device_ids=true, to_apply=%region_143.144.clone | all-reduce | flops 4096 | bytes 32768
  1172.3 22.4 %reduce-scatter.81.cloned.1.call-done = bf16[64,1024]{1,0:T(8,128)(2,1)} async-done(((bf16[256,1024]{1,0:T(8,128)(2,1)}), bf16[64,1024]{1,0:T(8,128)(2,1)}) %reduce-scatter.81.cloned.1.call-update) | async-done | bytes 131088 | tf_op jit(solution)/shard_map/reduce_scatter | solution.py:206
  1196.5 21.0 %reduce-scatter.85.cloned.1.call-done = bf16[256,256]{1,0:T(8,128)(2,1)} async-done(((bf16[256,1024]{1,0:T(8,128)(2,1)}), bf16[256,256]{1,0:T(8,128)(2,1)}) %reduce-scatter.85.cloned.1.call-update) | async-done | bytes 131088 | tf_op jit(solution)/shard_map/reduce_scatter | solution.py:296
  1219.1 32.1 %reduce-scatter.87.cloned.1.call-done = bf16[256,1024]{1,0:T(8,128)(2,1)} async-done(((bf16[1024,1024]{1,0:T(8,128)(2,1)}), bf16[256,1024]{1,0:T(8,128)(2,1)}) %reduce-scatter.87.cloned.1.call-update) | async-done | bytes 524304 | tf_op jit(solution)/shard_map/reduce_scatter | solution.py:299
  1253.3 31.6 %reduce-scatter.89.cloned.1.call-done = bf16[1024,256]{1,0:T(8,128)(2,1)} async-done(((bf16[1024,1024]{1,0:T(8,128)(2,1)}), bf16[1024,256]{1,0:T(8,128)(2,1)}) %reduce-scatter.89.cloned.1.call-update) | async-done | bytes 524304 | tf_op jit(solution)/shard_map/reduce_scatter | solution.py:302
  1287.0 28.4 %reduce-scatter.83.cloned.1.call-done = bf16[256,3,256]{2,0,1:T(8,128)(2,1)} async-done(((bf16[1024,3,256]{2,0,1:T(8,128)(2,1)}), bf16[256,3,256]{2,0,1:T(8,128)(2,1)}) %reduce-scatter.83.cloned.1.call-update) | async-done | bytes 393232 | tf_op jit(solution)/shard_map/reduce_scatter | solution.py:293
  (1211 shorter events, 603.4 us)
Async XLA Ops:
  9.2 61.0 %reduce-scatter.35.cloned.1.call-start = ((), (), s32[]{:S(2)}) async-start(), calls=%async_computation.30 | async-start | bytes 1310720 | tf_op jit(solution)/shard_map/reduce_scatter | solution.py:136
  41.8 51.2 %all-gather.11.cloned.1.call-start = ((), (), s32[]{:S(2)}) async-start(), calls=%async_computation.59 | async-start | bytes 2621440 | tf_op jit(solution)/shard_map/all_gather | solution.py:253
  42.5 74.7 %all-gather.13.cloned.1.call-start = ((), (), s32[]{:S(2)}) async-start(), calls=%async_computation.60 | async-start | bytes 2621440 | tf_op jit(solution)/shard_map/all_gather | solution.py:254
  43.1 99.2 %reduce-scatter.37.cloned.1.call-start = ((), (), s32[]{:S(2)}) async-start(), calls=%async_computation.31 | async-start | bytes 655360 | tf_op jit(solution)/shard_map/reduce_scatter | solution.py:144
  120.3 66.9 %reduce-scatter.55.cloned.1.call-start = ((), (), s32[]{:S(2)}) async-start(), calls=%async_computation.40 | async-start | bytes 655360 | tf_op jit(solution)/shard_map/reduce_scatter | solution.py:192
  166.8 77.3 %reduce-scatter.39.cloned.1.call-start = ((), (), s32[]{:S(2)}) async-start(), calls=%async_computation.32 | async-start | bytes 1310720 | tf_op jit(solution)/shard_map/reduce_scatter | solution.py:136
  216.7 94.3 %reduce-scatter.41.cloned.1.call-start = ((), (), s32[]{:S(2)}) async-start(), calls=%async_computation.33 | async-start | bytes 655360 | tf_op jit(solution)/shard_map/reduce_scatter | solution.py:144
  290.6 43.4 %reduce-scatter.57.cloned.1.call-start = ((), (), s32[]{:S(2)}) async-start(), calls=%async_computation.41 | async-start | bytes 655360 | tf_op jit(solution)/shard_map/reduce_scatter | solution.py:206
  297.9 99.6 %reduce-scatter.59.cloned.1.call-start = ((), (), s32[]{:S(2)}) async-start(), calls=%async_computation.42 | async-start | bytes 655360 | tf_op jit(solution)/shard_map/reduce_scatter | solution.py:192
  376.8 48.6 %reduce-scatter.43.cloned.1.call-start = ((), (), s32[]{:S(2)}) async-start(), calls=%async_computation.34 | async-start | bytes 1310720 | tf_op jit(solution)/shard_map/reduce_scatter | solution.py:136
  383.9 95.0 %reduce-scatter.45.cloned.1.call-start = ((), (), s32[]{:S(2)}) async-start(), calls=%async_computation.35 | async-start | bytes 655360 | tf_op jit(solution)/shard_map/reduce_scatter | solution.py:144
  451.6 61.8 %reduce-scatter.61.cloned.1.call-start = ((), (), s32[]{:S(2)}) async-start(), calls=%async_computation.43 | async-start | bytes 655360 | tf_op jit(solution)/shard_map/reduce_scatter | solution.py:206
  488.1 61.8 %reduce-scatter.47.cloned.1.call-start = ((), (), s32[]{:S(2)}) async-start(), calls=%async_computation.36 | async-start | bytes 1310720 | tf_op jit(solution)/shard_map/reduce_scatter | solution.py:136
  513.3 58.5 %reduce-scatter.63.cloned.1.call-start = ((), (), s32[]{:S(2)}) async-start(), calls=%async_computation.44 | async-start | bytes 655360 | tf_op jit(solution)/shard_map/reduce_scatter | solution.py:192
  549.8 66.8 %reduce-scatter.49.cloned.1.call-start = ((), (), s32[]{:S(2)}) async-start(), calls=%async_computation.37 | async-start | bytes 655360 | tf_op jit(solution)/shard_map/reduce_scatter | solution.py:144
  596.1 76.3 %reduce-scatter.51.cloned.1.call-start = ((), (), s32[]{:S(2)}) async-start(), calls=%async_computation.38 | async-start | bytes 1310720 | tf_op jit(solution)/shard_map/reduce_scatter | solution.py:136
  645.0 82.0 %reduce-scatter.53.cloned.1.call-start = ((), (), s32[]{:S(2)}) async-start(), calls=%async_computation.39 | async-start | bytes 655360 | tf_op jit(solution)/shard_map/reduce_scatter | solution.py:144
  698.3 60.3 %reduce-scatter.65.cloned.1.call-start = ((), (), s32[]{:S(2)}) async-start(), calls=%async_computation.45 | async-start | bytes 655360 | tf_op jit(solution)/shard_map/reduce_scatter | solution.py:206
  734.6 61.5 %reduce-scatter.75.cloned.1.call-start = ((), (), s32[]{:S(2)}) async-start(), calls=%async_computation.50 | async-start | bytes 1310720 | tf_op jit(solution)/shard_map/reduce_scatter | solution.py:136
  758.5 59.3 %reduce-scatter.67.cloned.1.call-start = ((), (), s32[]{:S(2)}) async-start(), calls=%async_computation.46 | async-start | bytes 655360 | tf_op jit(solution)/shard_map/reduce_scatter | solution.py:192
  794.2 75.0 %reduce-scatter.69.cloned.1.call-start = ((), (), s32[]{:S(2)}) async-start(), calls=%async_computation.47 | async-start | bytes 655360 | tf_op jit(solution)/shard_map/reduce_scatter | solution.py:206
  846.8 71.2 %reduce-scatter.77.cloned.1.call-start = ((), (), s32[]{:S(2)}) async-start(), calls=%async_computation.51 | async-start | bytes 655360 | tf_op jit(solution)/shard_map/reduce_scatter | solution.py:144
  877.7 53.3 %reduce-scatter.71.cloned.1.call-start = ((), (), s32[]{:S(2)}) async-start(), calls=%async_computation.48 | async-start | bytes 655360 | tf_op jit(solution)/shard_map/reduce_scatter | solution.py:192
  908.5 74.3 %reduce-scatter.73.cloned.1.call-start = ((), (), s32[]{:S(2)}) async-start(), calls=%async_computation.49 | async-start | bytes 655360 | tf_op jit(solution)/shard_map/reduce_scatter | solution.py:206
  962.4 71.3 %reduce-scatter.79.cloned.1.call-start = ((), (), s32[]{:S(2)}) async-start(), calls=%async_computation.52 | async-start | bytes 655360 | tf_op jit(solution)/shard_map/reduce_scatter | solution.py:192
  1013.7 147.5 %reduce-scatter.91.cloned.1.call-start = ((), (), s32[]{:S(2)}) async-start(), calls=%async_computation.61 | async-start | bytes 557056
  1057.3 113.6 %reduce-scatter.93.cloned.1.call-start = ((), (), s32[]{:S(2)}) async-start(), calls=%async_computation.62 | async-start | bytes 557056
  1060.2 134.4 %reduce-scatter.81.cloned.1.call-start = ((), (), s32[]{:S(2)}) async-start(), calls=%async_computation.53 | async-start | bytes 655360 | tf_op jit(solution)/shard_map/reduce_scatter | solution.py:206
  1062.8 154.7 %reduce-scatter.85.cloned.1.call-start = ((), (), s32[]{:S(2)}) async-start(), calls=%async_computation.55 | async-start | bytes 655360 | tf_op jit(solution)/shard_map/reduce_scatter | solution.py:296
  1069.9 181.3 %reduce-scatter.87.cloned.1.call-start = ((), (), s32[]{:S(2)}) async-start(), calls=%async_computation.56 | async-start | bytes 2621440 | tf_op jit(solution)/shard_map/reduce_scatter | solution.py:299
  1080.0 204.9 %reduce-scatter.89.cloned.1.call-start = ((), (), s32[]{:S(2)}) async-start(), calls=%async_computation.57 | async-start | bytes 2621440 | tf_op jit(solution)/shard_map/reduce_scatter | solution.py:302
  1091.6 223.8 %reduce-scatter.83.cloned.1.call-start = ((), (), s32[]{:S(2)}) async-start(), calls=%async_computation.54 | async-start | bytes 1966080 | tf_op jit(solution)/shard_map/reduce_scatter | solution.py:293
  (392 other events, 4531.6 us)
Sparse Core Ops, SparseCore 0:
  10.1 22.6 all-gather.8
  41.9 28.3 reduce-scatter.34
  71.8 21.0 all-gather.10
  94.3 22.8 all-gather.12
  120.4 21.8 reduce-scatter.36
  166.9 20.2 reduce-scatter.54
  216.8 27.2 reduce-scatter.38
  290.7 20.2 reduce-scatter.40
  313.9 20.1 reduce-scatter.56
  376.9 20.5 reduce-scatter.58
  399.8 25.5 reduce-scatter.42
  451.7 22.2 reduce-scatter.44
  488.2 21.2 reduce-scatter.60
  513.5 35.2 reduce-scatter.46
  551.5 20.3 reduce-scatter.62
  596.2 20.2 reduce-scatter.48
  645.2 27.2 reduce-scatter.50
  698.4 21.8 reduce-scatter.52
  734.7 21.0 reduce-scatter.64
  758.6 35.9 reduce-scatter.74
  797.4 20.2 reduce-scatter.66
  846.9 22.0 reduce-scatter.68
  877.9 25.8 reduce-scatter.76
  908.6 22.3 reduce-scatter.70
  962.5 20.2 reduce-scatter.72
  1057.4 54.6 reduce-scatter.90
  1115.6 55.2 reduce-scatter.92
  1173.7 20.8 reduce-scatter.80
  1197.5 19.8 reduce-scatter.84
  1220.0 31.1 reduce-scatter.86
  1253.7 31.1 reduce-scatter.88
  1287.3 28.0 reduce-scatter.82
  (1 shorter events, 19.7 us)
where the time goes:
time: 1340 us; the launch traced here: 1320 us
  waiting for transfers between devices  477 us (36%)
  blocking collectives  467 us (35%)
  matrix products  163 us (12%)
  other arithmetic  113 us (8%)
  local copies, waits for them, and re-layouts  58.1 us (4%)
  starting transfers between devices  25.9 us (2%)
  between operations  20.3 us (2%)
    all_gather x6, blocking collectives, layer_backward(): lax.all_gather(grad_second.astype(jnp.bfloat16), 'tensor', axis=0, tiled=...  108 us
    reduce_scatter x6, waiting for transfers between devices, layer_forward(): lax.psum_scatter(partial_value, 'tensor', scatter_dimension=0, tiled=True)  106 us
    reduce_scatter x6, waiting for transfers between devices, layer_backward(): lax.psum_scatter(grad_spread.astype(jnp.bfloat16), 'tensor', scatter_dime...  98.7 us
    all_gather x6, blocking collectives, layer_backward(): lax.all_gather(grad_first.astype(jnp.bfloat16), 'tensor', axis=0, tiled=T...  98.5 us
    all_gather x6, blocking collectives, layer_forward(): gathered = lax.all_gather(current, 'tensor', axis=0, tiled=True)  97.8 us
    all_gather x6, blocking collectives, layer_forward(): lax.all_gather(normed.astype(jnp.bfloat16), 'tensor', axis=0, tiled=True)  97 us
    unnamed x1, blocking collectives  58.1 us
    reduce_scatter x6, waiting for transfers between devices, layer_forward(): lax.psum_scatter(partial_out.astype(jnp.bfloat16), 'tensor', scatter_dime...  54 us
  transfers between devices with their start and end apart: 43, of which 31 were waited for; matrix products, arithmetic and copies ran while one was open for 13% of the time, Pallas kernels for 0%

commit v1 on v0

--- a/solution.py
+++ b/solution.py
@@ -183,7 +183,16 @@
     ) = kept_state
     w_qkv, w_o, w_in, w_out = weights
     grad_second, gain_two, shift_two = norm_backward(upstream, scaled_two, inverse_two, gains[1])
-    grad_feed = lax.all_gather(grad_second.astype(jnp.bfloat16), "tensor", axis=0, tiled=True)
+    shard = grad_second.astype(jnp.bfloat16)
+    ways, here, step = (lax.axis_size("tensor"), lax.axis_index("tensor"), shard.shape[0])
+    line, have = (shard, 1)
+    while have < ways:
+        line = jnp.concatenate(
+            [line, lax.ppermute(line, "tensor", [(d, (d - have) % ways) for d in range(ways)])],
+            axis=0,
+        )
+        have = 2 * have
+    grad_feed = jnp.roll(line, here * step, axis=0)
     grad_active = dot_cols(grad_feed, w_out)
     grad_w_out = dot_rows(active, grad_feed)
     grad_hidden = (grad_active * gelu_slope(hidden)).astype(jnp.bfloat16)

time: 1340 us -> 1410 us (1.052)
  waiting for transfers between devices: 477 us -> 659 us
  blocking collectives: 467 us -> 350 us
    all_gather x6 -> x0, blocking collectives: 108 us -> none  [layer_backward(): lax.all_gather(grad_second.astype(jnp.bfloat16), 'tensor', axis=0, tiled=...]
    ppermute x0 -> x12, waiting for transfers between devices: none -> 102 us  [layer_backward(): lax.ppermute(line, 'tensor', [(d, (d - have) % ways) for d in range(ways)])]
    reduce_scatter x6, waiting for transfers between devices: 51.7 us -> 107 us  [layer_backward(): lax.psum_scatter(grad_gathered.astype(jnp.bfloat16), 'tensor', scatter_di...]
    reduce_scatter x6, waiting for transfers between devices: 98.7 us -> 120 us  [layer_backward(): lax.psum_scatter(grad_spread.astype(jnp.bfloat16), 'tensor', scatter_dime...]
    reduce_scatter x6, waiting for transfers between devices: 54 us -> 70.3 us  [layer_forward(): lax.psum_scatter(partial_out.astype(jnp.bfloat16), 'tensor', scatter_dime...]
    unnamed x770 -> x836, local copies, waits for them, and re-layouts: 39.2 us -> 39.4 us
  transfers between devices with their start and end apart: 43 -> 55, of which waited for: 31 -> 43; matrix products, arithmetic and copies ran while one was open for 13% -> 12% of each run, Pallas kernels for 0% -> 0%
where the time goes in v1:
time: 1410 us; the launch traced here: 1400 us
  waiting for transfers between devices  659 us (47%)
  blocking collectives  350 us (25%)
  matrix products  156 us (11%)
  other arithmetic  120 us (9%)
  local copies, waits for them, and re-layouts  56.7 us (4%)
  starting transfers between devices  34.8 us (2%)
  between operations  20.9 us (1%)
    reduce_scatter x6, waiting for transfers between devices, layer_backward(): lax.psum_scatter(grad_spread.astype(jnp.bfloat16), 'tensor', scatter_dime...  120 us
    reduce_scatter x6, waiting for transfers between devices, layer_backward(): lax.psum_scatter(grad_gathered.astype(jnp.bfloat16), 'tensor', scatter_di...  107 us
    reduce_scatter x6, waiting for transfers between devices, layer_forward(): lax.psum_scatter(partial_value, 'tensor', scatter_dimension=0, tiled=True)  105 us
    ppermute x12, waiting for transfers between devices, layer_backward(): lax.ppermute(line, 'tensor', [(d, (d - have) % ways) for d in range(ways)])  102 us
    all_gather x6, blocking collectives, layer_backward(): lax.all_gather(grad_first.astype(jnp.bfloat16), 'tensor', axis=0, tiled=T...  96.4 us
    all_gather x6, blocking collectives, layer_forward(): lax.all_gather(normed.astype(jnp.bfloat16), 'tensor', axis=0, tiled=True)  94.4 us
    all_gather x6, blocking collectives, layer_forward(): gathered = lax.all_gather(current, 'tensor', axis=0, tiled=True)  93.6 us
    reduce_scatter x6, waiting for transfers between devices, layer_forward(): lax.psum_scatter(partial_out.astype(jnp.bfloat16), 'tensor', scatter_dime...  70.3 us
  transfers between devices with their start and end apart: 55, of which 43 were waited for; matrix products, arithmetic and copies ran while one was open for 12% of the time, Pallas kernels for 0%

profile of v1, /device:TPU:0, one launch (start us, length us, event | category | flops | bytes accessed | tf_op | source)
XLA Modules:
  0.0 1396.7 jit_solution(17312022730181873107)
XLA Ops:
  11.2 17.4 %all-gather = bf16[1,256,1024]{2,1,0:T(8,128)(2,1)S(1)} all-gather(bf16[1,64,1024]{2,1,0:T(8,128)(2,1)S(1)} %slice_select_fusion), channel_id=2, replica_groups=mesh['pipe'=2,'dp'=4,'tensor'=4] {'tensor'}, dimensions={1}, use_global_device_ids=true | all-gather | bytes 655360 | tf_op jit(solution)/shard_map/all_gather | solution.py:129
  42.6 27.1 %reduce-scatter.35.cloned.1.call-done = f32[64,1024]{1,0:T(8,128)} async-done(((f32[256,1024]{1,0:T(8,128)}), f32[64,1024]{1,0:T(8,128)}) %reduce-scatter.35.cloned.1.call-update) | async-done | bytes 262160 | tf_op jit(solution)/shard_map/reduce_scatter | solution.py:136
  73.0 16.0 %all_gather.89 = bf16[256,1024]{1,0:T(8,128)(2,1)S(1)} all-gather(bf16[64,1024]{1,0:T(8,128)(2,1)S(1)} %get-tuple-element.419), channel_id=1, replica_groups=mesh['pipe'=2,'dp'=4,'tensor'=4] {'tensor'}, dimensions={0}, use_global_device_ids=true | all-gather | bytes 655360 | tf_op jit(solution)/shard_map/all_gather | solution.py:140
  97.7 18.8 %all-gather.13.cloned.1.call-done = bf16[1,1024,1024]{2,1,0:T(8,128)(2,1)} async-done(((bf16[1,1024,256]{2,1,0:T(8,128)(2,1)}), bf16[1,1024,1024]{2,1,0:T(8,128)(2,1)}) %all-gather.13.cloned.1.call-update) | async-done | bytes 2097168 | tf_op jit(solution)/shard_map/all_gather | solution.py:263
  121.0 20.7 %reduce-scatter.37.cloned.1.call-done = bf16[64,1024]{1,0:T(8,128)(2,1)} async-done(((bf16[256,1024]{1,0:T(8,128)(2,1)}), bf16[64,1024]{1,0:T(8,128)(2,1)}) %reduce-scatter.37.cloned.1.call-update) | async-done | bytes 131088 | tf_op jit(solution)/shard_map/reduce_scatter | solution.py:144
  170.3 20.7 %reduce-scatter.55.cloned.1.call-done = bf16[64,1024]{1,0:T(8,128)(2,1)} async-done(((bf16[256,1024]{1,0:T(8,128)(2,1)}), bf16[64,1024]{1,0:T(8,128)(2,1)}) %reduce-scatter.55.cloned.1.call-update) | async-done | bytes 131088 | tf_op jit(solution)/shard_map/reduce_scatter | solution.py:201
  222.4 26.2 %reduce-scatter.39.cloned.1.call-done = f32[64,1024]{1,0:T(8,128)} async-done(((f32[256,1024]{1,0:T(8,128)}), f32[64,1024]{1,0:T(8,128)}) %reduce-scatter.39.cloned.1.call-update) | async-done | bytes 262160 | tf_op jit(solution)/shard_map/reduce_scatter | solution.py:136
  254.0 16.1 %all_gather.100 = bf16[256,1024]{1,0:T(8,128)(2,1)S(1)} all-gather(bf16[64,1024]{1,0:T(8,128)(2,1)S(1)} %convert_element_type.638), channel_id=1, replica_groups=mesh['pipe'=2,'dp'=4,'tensor'=4] {'tensor'}, dimensions={0}, use_global_device_ids=true | all-gather | bytes 655360 | tf_op jit(solution)/shard_map/all_gather | solution.py:205
  273.4 15.6 %all_gather.93 = bf16[256,1024]{1,0:T(8,128)(2,1)S(1)} all-gather(bf16[64,1024]{1,0:T(8,128)(2,1)S(1)} %get-tuple-element.479), channel_id=1, replica_groups=mesh['pipe'=2,'dp'=4,'tensor'=4] {'tensor'}, dimensions={0}, use_global_device_ids=true | all-gather | bytes 655360 | tf_op jit(solution)/shard_map/all_gather | solution.py:140
  317.0 21.7 %reduce-scatter.57.cloned.1.call-done = bf16[64,1024]{1,0:T(8,128)(2,1)} async-done(((bf16[256,1024]{1,0:T(8,128)(2,1)}), bf16[64,1024]{1,0:T(8,128)(2,1)}) %reduce-scatter.57.cloned.1.call-update) | async-done | bytes 131088 | tf_op jit(solution)/shard_map/reduce_scatter | solution.py:215
  350.1 15.9 %all_gather.94 = bf16[256,1024]{1,0:T(8,128)(2,1)S(1)} all-gather(bf16[64,1024]{1,0:T(8,128)(2,1)S(1)} %bitcast_select_fusion.7), channel_id=1, replica_groups=mesh['pipe'=2,'dp'=4,'tensor'=4] {'tensor'}, dimensions={0}, use_global_device_ids=true | all-gather | bytes 655360 | tf_op jit(solution)/shard_map/all_gather | solution.py:129
  406.1 26.2 %reduce-scatter.43.cloned.1.call-done = f32[64,1024]{1,0:T(8,128)} async-done(((f32[256,1024]{1,0:T(8,128)}), f32[64,1024]{1,0:T(8,128)}) %reduce-scatter.43.cloned.1.call-update) | async-done | bytes 262160 | tf_op jit(solution)/shard_map/reduce_scatter | solution.py:136
  436.7 15.9 %all_gather.101 = bf16[256,1024]{1,0:T(8,128)(2,1)S(1)} all-gather(bf16[64,1024]{1,0:T(8,128)(2,1)S(1)} %convert_element_type.649), channel_id=1, replica_groups=mesh['pipe'=2,'dp'=4,'tensor'=4] {'tensor'}, dimensions={0}, use_global_device_ids=true | all-gather | bytes 655360 | tf_op jit(solution)/shard_map/all_gather | solution.py:205
  456.8 15.6 %all_gather.95 = bf16[256,1024]{1,0:T(8,128)(2,1)S(1)} all-gather(bf16[64,1024]{1,0:T(8,128)(2,1)S(1)} %get-tuple-element.478), channel_id=1, replica_groups=mesh['pipe'=2,'dp'=4,'tensor'=4] {'tensor'}, dimensions={0}, use_global_device_ids=true | all-gather | bytes 655360 | tf_op jit(solution)/shard_map/all_gather | solution.py:140
  506.4 15.6 %reduce-scatter.61.cloned.1.call-done = bf16[64,1024]{1,0:T(8,128)(2,1)} async-done(((bf16[256,1024]{1,0:T(8,128)(2,1)}), bf16[64,1024]{1,0:T(8,128)(2,1)}) %reduce-scatter.61.cloned.1.call-update) | async-done | bytes 131088 | tf_op jit(solution)/shard_map/reduce_scatter | solution.py:215
  556.4 22.9 %collective-permute-done.11 = bf16[128,1024]{1,0:T(8,128)(2,1)S(1)} collective-permute-done((bf16[128,1024]{1,0:T(8,128)(2,1)S(1)}, bf16[128,1024]{1,0:T(8,128)(2,1)S(1)}, u32[]{:S(2)}, u32[]{:S(2)}) %collective-permute-start.11) | collective-permute-done | bytes 262176 | tf_op jit(solution)/shard_map/ppermute | solution.py:191
  587.8 21.7 %reduce-scatter.63.cloned.1.call-done = bf16[64,1024]{1,0:T(8,128)(2,1)} async-done(((bf16[256,1024]{1,0:T(8,128)(2,1)}), bf16[64,1024]{1,0:T(8,128)(2,1)}) %reduce-scatter.63.cloned.1.call-update) | async-done | bytes 131088 | tf_op jit(solution)/shard_map/reduce_scatter | solution.py:201
  634.0 20.3 %reduce-scatter.49.cloned.1.call-done = bf16[64,1024]{1,0:T(8,128)(2,1)} async-done(((bf16[256,1024]{1,0:T(8,128)(2,1)}), bf16[64,1024]{1,0:T(8,128)(2,1)}) %reduce-scatter.49.cloned.1.call-update) | async-done | bytes 131088 | tf_op jit(solution)/shard_map/reduce_scatter | solution.py:144
  685.0 25.1 %reduce-scatter.51.cloned.1.call-done = f32[64,1024]{1,0:T(8,128)} async-done(((f32[256,1024]{1,0:T(8,128)}), f32[64,1024]{1,0:T(8,128)}) %reduce-scatter.51.cloned.1.call-update) | async-done | bytes 262160 | tf_op jit(solution)/shard_map/reduce_scatter | solution.py:136
  713.5 15.9 %all_gather.99 = bf16[256,1024]{1,0:T(8,128)(2,1)S(1)} all-gather(bf16[64,1024]{1,0:T(8,128)(2,1)S(1)} %get-tuple-element.476), channel_id=1, replica_groups=mesh['pipe'=2,'dp'=4,'tensor'=4] {'tensor'}, dimensions={0}, use_global_device_ids=true | all-gather | bytes 655360 | tf_op jit(solution)/shard_map/all_gather | solution.py:140
  736.5 18.2 %all_gather.102 = bf16[256,1024]{1,0:T(8,128)(2,1)S(1)} all-gather(bf16[64,1024]{1,0:T(8,128)(2,1)S(1)} %convert_element_type.661), channel_id=1, replica_groups=mesh['pipe'=2,'dp'=4,'tensor'=4] {'tensor'}, dimensions={0}, use_global_device_ids=true | all-gather | bytes 655360 | tf_op jit(solution)/shard_map/all_gather | solution.py:205
  819.9 22.5 %collective-permute-done.14 = bf16[128,1024]{1,0:T(8,128)(2,1)S(1)} collective-permute-done((bf16[128,1024]{1,0:T(8,128)(2,1)S(1)}, bf16[128,1024]{1,0:T(8,128)(2,1)S(1)}, u32[]{:S(2)}, u32[]{:S(2)}) %collective-permute-start.14) | collective-permute-done | bytes 262176 | tf_op jit(solution)/shard_map/ppermute | solution.py:191
  850.8 23.5 %reduce-scatter.67.cloned.1.call-done = bf16[64,1024]{1,0:T(8,128)(2,1)} async-done(((bf16[256,1024]{1,0:T(8,128)(2,1)}), bf16[64,1024]{1,0:T(8,128)(2,1)}) %reduce-scatter.67.cloned.1.call-update) | async-done | bytes 131088 | tf_op jit(solution)/shard_map/reduce_scatter | solution.py:201
  903.1 20.4 %reduce-scatter.69.cloned.1.call-done = bf16[64,1024]{1,0:T(8,128)(2,1)} async-done(((bf16[256,1024]{1,0:T(8,128)(2,1)}), bf16[64,1024]{1,0:T(8,128)(2,1)}) %reduce-scatter.69.cloned.1.call-update) | async-done | bytes 131088 | tf_op jit(solution)/shard_map/reduce_scatter | solution.py:215
  926.6 15.9 %all_gather.106 = bf16[256,1024]{1,0:T(8,128)(2,1)S(1)} all-gather(bf16[64,1024]{1,0:T(8,128)(2,1)} %get-tuple-element.465), channel_id=1, replica_groups=mesh['pipe'=2,'dp'=4,'tensor'=4] {'tensor'}, dimensions={0}, use_global_device_ids=true | all-gather | bytes 655360 | tf_op jit(solution)/shard_map/all_gather | solution.py:140
  980.1 22.8 %reduce-scatter.71.cloned.1.call-done = bf16[64,1024]{1,0:T(8,128)(2,1)} async-done(((bf16[256,1024]{1,0:T(8,128)(2,1)}), bf16[64,1024]{1,0:T(8,128)(2,1)}) %reduce-scatter.71.cloned.1.call-update) | async-done | bytes 131088 | tf_op jit(solution)/shard_map/reduce_scatter | solution.py:201
  1173.9 58.0 %all-reduce = f32[4096]{0:T(1024)S(1)} all-reduce(f32[4096]{0:T(1024)S(1)} %add_dynamic-update-slice_fusion), channel_id=37, replica_groups=mesh['pipe'=2,'dp'=4,'tensor'=4] {'dp','tensor'}, use_global_device_ids=true, to_apply=%region_143.145.clone | all-reduce | flops 4096 | bytes 32768
  1244.6 22.3 %reduce-scatter.81.cloned.1.call-done = bf16[64,1024]{1,0:T(8,128)(2,1)} async-done(((bf16[256,1024]{1,0:T(8,128)(2,1)}), bf16[64,1024]{1,0:T(8,128)(2,1)}) %reduce-scatter.81.cloned.1.call-update) | async-done | bytes 131088 | tf_op jit(solution)/shard_map/reduce_scatter | solution.py:215
  1268.8 21.0 %reduce-scatter.85.cloned.1.call-done = bf16[256,256]{1,0:T(8,128)(2,1)} async-done(((bf16[256,1024]{1,0:T(8,128)(2,1)}), bf16[256,256]{1,0:T(8,128)(2,1)}) %reduce-scatter.85.cloned.1.call-update) | async-done | bytes 131088 | tf_op jit(solution)/shard_map/reduce_scatter | solution.py:305
  1291.4 32.1 %reduce-scatter.87.cloned.1.call-done = bf16[256,1024]{1,0:T(8,128)(2,1)} async-done(((bf16[1024,1024]{1,0:T(8,128)(2,1)}), bf16[256,1024]{1,0:T(8,128)(2,1)}) %reduce-scatter.87.cloned.1.call-update) | async-done | bytes 524304 | tf_op jit(solution)/shard_map/reduce_scatter | solution.py:308
  1325.7 31.6 %reduce-scatter.89.cloned.1.call-done = bf16[1024,256]{1,0:T(8,128)(2,1)} async-done(((bf16[1024,1024]{1,0:T(8,128)(2,1)}), bf16[1024,256]{1,0:T(8,128)(2,1)}) %reduce-scatter.89.cloned.1.call-update) | async-done | bytes 524304 | tf_op jit(solution)/shard_map/reduce_scatter | solution.py:311
  1359.3 28.4 %reduce-scatter.83.cloned.1.call-done = bf16[256,3,256]{2,0,1:T(8,128)(2,1)} async-done(((bf16[1024,3,256]{2,0,1:T(8,128)(2,1)}), bf16[256,3,256]{2,0,1:T(8,128)(2,1)}) %reduce-scatter.83.cloned.1.call-update) | async-done | bytes 393232 | tf_op jit(solution)/shard_map/reduce_scatter | solution.py:302
  (1307 shorter events, 663.7 us)
Async XLA Ops:
  9.2 60.4 %reduce-scatter.35.cloned.1.call-start = ((), (), s32[]{:S(2)}) async-start(), calls=%async_computation.30 | async-start | bytes 1310720 | tf_op jit(solution)/shard_map/reduce_scatter | solution.py:136
  41.1 51.2 %all-gather.11.cloned.1.call-start = ((), (), s32[]{:S(2)}) async-start(), calls=%async_computation.59 | async-start | bytes 2621440 | tf_op jit(solution)/shard_map/all_gather | solution.py:262
  41.9 74.7 %all-gather.13.cloned.1.call-start = ((), (), s32[]{:S(2)}) async-start(), calls=%async_computation.60 | async-start | bytes 2621440 | tf_op jit(solution)/shard_map/all_gather | solution.py:263
  42.5 99.2 %reduce-scatter.37.cloned.1.call-start = ((), (), s32[]{:S(2)}) async-start(), calls=%async_computation.31 | async-start | bytes 655360 | tf_op jit(solution)/shard_map/reduce_scatter | solution.py:144
  119.7 71.3 %reduce-scatter.55.cloned.1.call-start = ((), (), s32[]{:S(2)}) async-start(), calls=%async_computation.40 | async-start | bytes 655360 | tf_op jit(solution)/shard_map/reduce_scatter | solution.py:201
  169.6 79.0 %reduce-scatter.39.cloned.1.call-start = ((), (), s32[]{:S(2)}) async-start(), calls=%async_computation.32 | async-start | bytes 1310720 | tf_op jit(solution)/shard_map/reduce_scatter | solution.py:136
  221.2 94.5 %reduce-scatter.41.cloned.1.call-start = ((), (), s32[]{:S(2)}) async-start(), calls=%async_computation.33 | async-start | bytes 655360 | tf_op jit(solution)/shard_map/reduce_scatter | solution.py:144
  295.2 43.4 %reduce-scatter.57.cloned.1.call-start = ((), (), s32[]{:S(2)}) async-start(), calls=%async_computation.41 | async-start | bytes 655360 | tf_op jit(solution)/shard_map/reduce_scatter | solution.py:215
  302.5 101.9 %reduce-scatter.59.cloned.1.call-start = ((), (), s32[]{:S(2)}) async-start(), calls=%async_computation.42 | async-start | bytes 655360 | tf_op jit(solution)/shard_map/reduce_scatter | solution.py:201
  383.2 49.0 %reduce-scatter.43.cloned.1.call-start = ((), (), s32[]{:S(2)}) async-start(), calls=%async_computation.34 | async-start | bytes 1310720 | tf_op jit(solution)/shard_map/reduce_scatter | solution.py:136
  388.0 111.1 %reduce-scatter.45.cloned.1.call-start = ((), (), s32[]{:S(2)}) async-start(), calls=%async_computation.35 | async-start | bytes 655360 | tf_op jit(solution)/shard_map/reduce_scatter | solution.py:144
  478.7 43.4 %reduce-scatter.61.cloned.1.call-start = ((), (), s32[]{:S(2)}) async-start(), calls=%async_computation.43 | async-start | bytes 655360 | tf_op jit(solution)/shard_map/reduce_scatter | solution.py:215
  486.0 100.5 %reduce-scatter.47.cloned.1.call-start = ((), (), s32[]{:S(2)}) async-start(), calls=%async_computation.36 | async-start | bytes 1310720 | tf_op jit(solution)/shard_map/reduce_scatter | solution.py:136
  546.0 63.5 %reduce-scatter.63.cloned.1.call-start = ((), (), s32[]{:S(2)}) async-start(), calls=%async_computation.44 | async-start | bytes 655360 | tf_op jit(solution)/shard_map/reduce_scatter | solution.py:201
  586.4 67.9 %reduce-scatter.49.cloned.1.call-start = ((), (), s32[]{:S(2)}) async-start(), calls=%async_computation.37 | async-start | bytes 655360 | tf_op jit(solution)/shard_map/reduce_scatter | solution.py:144
  633.9 76.1 %reduce-scatter.51.cloned.1.call-start = ((), (), s32[]{:S(2)}) async-start(), calls=%async_computation.38 | async-start | bytes 1310720 | tf_op jit(solution)/shard_map/reduce_scatter | solution.py:136
  682.6 84.1 %reduce-scatter.53.cloned.1.call-start = ((), (), s32[]{:S(2)}) async-start(), calls=%async_computation.39 | async-start | bytes 655360 | tf_op jit(solution)/shard_map/reduce_scatter | solution.py:144
  736.4 51.2 %reduce-scatter.65.cloned.1.call-start = ((), (), s32[]{:S(2)}) async-start(), calls=%async_computation.45 | async-start | bytes 655360 | tf_op jit(solution)/shard_map/reduce_scatter | solution.py:215
  766.6 82.3 %reduce-scatter.75.cloned.1.call-start = ((), (), s32[]{:S(2)}) async-start(), calls=%async_computation.50 | async-start | bytes 1310720 | tf_op jit(solution)/shard_map/reduce_scatter | solution.py:136
  809.9 64.4 %reduce-scatter.67.cloned.1.call-start = ((), (), s32[]{:S(2)}) async-start(), calls=%async_computation.46 | async-start | bytes 655360 | tf_op jit(solution)/shard_map/reduce_scatter | solution.py:201
  848.0 75.5 %reduce-scatter.69.cloned.1.call-start = ((), (), s32[]{:S(2)}) async-start(), calls=%async_computation.47 | async-start | bytes 655360 | tf_op jit(solution)/shard_map/reduce_scatter | solution.py:215
  903.1 77.1 %reduce-scatter.77.cloned.1.call-start = ((), (), s32[]{:S(2)}) async-start(), calls=%async_computation.51 | async-start | bytes 655360 | tf_op jit(solution)/shard_map/reduce_scatter | solution.py:144
  956.6 46.3 %reduce-scatter.71.cloned.1.call-start = ((), (), s32[]{:S(2)}) async-start(), calls=%async_computation.48 | async-start | bytes 655360 | tf_op jit(solution)/shard_map/reduce_scatter | solution.py:201
  970.3 82.5 %reduce-scatter.73.cloned.1.call-start = ((), (), s32[]{:S(2)}) async-start(), calls=%async_computation.49 | async-start | bytes 655360 | tf_op jit(solution)/shard_map/reduce_scatter | solution.py:215
  1032.5 73.9 %reduce-scatter.79.cloned.1.call-start = ((), (), s32[]{:S(2)}) async-start(), calls=%async_computation.52 | async-start | bytes 655360 | tf_op jit(solution)/shard_map/reduce_scatter | solution.py:201
  1085.2 147.4 %reduce-scatter.91.cloned.1.call-start = ((), (), s32[]{:S(2)}) async-start(), calls=%async_computation.61 | async-start | bytes 557056
  1129.6 113.6 %reduce-scatter.93.cloned.1.call-start = ((), (), s32[]{:S(2)}) async-start(), calls=%async_computation.62 | async-start | bytes 557056
  1132.5 134.4 %reduce-scatter.81.cloned.1.call-start = ((), (), s32[]{:S(2)}) async-start(), calls=%async_computation.53 | async-start | bytes 655360 | tf_op jit(solution)/shard_map/reduce_scatter | solution.py:215
  1134.0 155.8 %reduce-scatter.85.cloned.1.call-start = ((), (), s32[]{:S(2)}) async-start(), calls=%async_computation.55 | async-start | bytes 655360 | tf_op jit(solution)/shard_map/reduce_scatter | solution.py:305
  1141.2 182.3 %reduce-scatter.87.cloned.1.call-start = ((), (), s32[]{:S(2)}) async-start(), calls=%async_computation.56 | async-start | bytes 2621440 | tf_op jit(solution)/shard_map/reduce_scatter | solution.py:308
  1151.4 205.8 %reduce-scatter.89.cloned.1.call-start = ((), (), s32[]{:S(2)}) async-start(), calls=%async_computation.57 | async-start | bytes 2621440 | tf_op jit(solution)/shard_map/reduce_scatter | solution.py:311
  1162.9 224.8 %reduce-scatter.83.cloned.1.call-start = ((), (), s32[]{:S(2)}) async-start(), calls=%async_computation.54 | async-start | bytes 1966080 | tf_op jit(solution)/shard_map/reduce_scatter | solution.py:302
  (437 other events, 5569.4 us)
Sparse Core Ops, SparseCore 0:
  10.1 22.5 all-gather.8
  41.3 28.3 reduce-scatter.34
  71.2 21.0 all-gather.10
  93.7 22.8 all-gather.12
  119.8 21.8 reduce-scatter.36
  169.7 21.2 reduce-scatter.54
  221.3 27.2 reduce-scatter.38
  295.4 20.2 reduce-scatter.40
  318.5 20.1 reduce-scatter.56
  383.3 21.0 reduce-scatter.58
  406.7 25.5 reduce-scatter.42
  478.8 20.2 reduce-scatter.44
  501.9 20.0 reduce-scatter.60
  546.2 35.1 reduce-scatter.46
  586.5 23.0 reduce-scatter.62
  634.1 20.1 reduce-scatter.48
  682.7 27.3 reduce-scatter.50
  736.5 21.8 reduce-scatter.52
  766.8 20.8 reduce-scatter.64
  810.0 34.8 reduce-scatter.74
  848.2 26.0 reduce-scatter.66
  903.2 20.2 reduce-scatter.68
  956.7 23.3 reduce-scatter.76
  982.8 20.0 reduce-scatter.70
  1032.6 20.2 reduce-scatter.72
  1085.3 21.0 reduce-scatter.78
  1129.7 54.6 reduce-scatter.90
  1188.0 55.1 reduce-scatter.92
  1246.1 20.8 reduce-scatter.80
  1292.3 31.1 reduce-scatter.86
  1326.1 31.1 reduce-scatter.88
  1359.6 28.0 reduce-scatter.82
  (1 shorter events, 19.9 us)
